TPU v7x, 32 devices: a whole 2x2x4 slice. The times are simulated.
32 devices in a mesh: grp: 4 (over x, core), seq: 8 (over z, y).
Axes of the slice: x: 2, y: 2, z: 4, core: 2. Of those that a mesh axis runs over, the one named last changes fastest.
Arguments:
- queries: bfloat16 [12288, 4096], P(('grp', 'seq')), may hold values from -6 to 6
- keys: bfloat16 [12288, 4096], P(('grp', 'seq')), may hold values from -6 to 6
- values: bfloat16 [12288, 4096], P(('grp', 'seq')), may hold values from -6 to 6
- gain: bfloat16 [4096], replicated, may hold values from 0.5 to 1.5
Outputs:
- attended: bfloat16 [12288, 4096], P(('grp', 'seq'))
All inputs are finite; a program needn't handle non-finite values.
Results may differ from a plain program's by a relative error of at most 0.0053.
Values sent between devices are 32-bit elements; how exact they have to be, the bound alone decides.
No kernel may reach another device: no remote copies, remote signals or barrier semaphores. Data moves between devices by JAX's collectives and lax.ppermute only.
A program may use at most 256 MiB of HBM per device.

v0:
```python
import jax
import jax.numpy as jnp
from jax import lax
from jax.sharding import PartitionSpec as P

HEADS = 32
HEAD_DIM = 128


def entering(value, axis, join, neutral):
    count, mine = (lax.axis_size(axis), lax.axis_index(axis))
    pieces = lax.all_gather(value, axis)
    subtotal = jnp.full_like(value, 0) + jnp.asarray(neutral, value.dtype)

    def lap(position, subtotal):
        longer = join(subtotal, pieces[position])
        return jnp.where(position < mine, longer, subtotal)

    return lax.fori_loop(0, count - 1, lap, subtotal)


def combine_sum(earlier, later):
    return earlier + later


def shards(queries, keys, values, gain):
    rows = queries.shape[0]
    fq = (
        jax.nn.silu(queries.astype(jnp.float32)).astype(jnp.bfloat16).reshape(rows, HEADS, HEAD_DIM)
    )
    fk = jax.nn.silu(keys.astype(jnp.float32)).astype(jnp.bfloat16).reshape(rows, HEADS, HEAD_DIM)
    vals = values.reshape(rows, HEADS, HEAD_DIM)
    local = jnp.einsum("thd,the->hde", fk, vals, preferred_element_type=jnp.float32)
    empty = jnp.zeros((HEADS, HEAD_DIM, HEAD_DIM), jnp.float32)
    within = entering(local, "seq", combine_sum, empty)
    total = lax.psum(local, "seq")
    before = entering(total, "grp", combine_sum, empty)
    carried = before + within
    positions = jnp.arange(rows, dtype=jnp.int32)
    causal = positions[:, None] >= positions[None, :]
    scores = jnp.einsum("thd,shd->hts", fq, fk, preferred_element_type=jnp.float32)
    scores = jnp.where(causal[None], scores, 0.0).astype(jnp.bfloat16)
    intra = jnp.einsum("hts,she->the", scores, vals, preferred_element_type=jnp.float32)
    inter = jnp.einsum(
        "thd,hde->the", fq, carried.astype(jnp.bfloat16), preferred_element_type=jnp.float32
    )
    mixed = intra + inter
    meansq = jnp.mean(mixed * mixed, axis=-1, keepdims=True)
    gains = gain.astype(jnp.float32).reshape(HEADS, HEAD_DIM)
    normed = mixed * lax.rsqrt(meansq + 1e-06) * gains[None]
    return normed.reshape(rows, HEADS * HEAD_DIM).astype(jnp.bfloat16)


def solution(mesh):
    return jax.shard_map(
        shards,
        mesh=mesh,
        in_specs=(P(("grp", "seq"), None), P(("grp", "seq"), None), P(("grp", "seq"), None), P()),
        out_specs=P(("grp", "seq"), None),
        check_vma=False,
    )
```

profile of v0, /device:TPU:0, one launch (start us, length us, event | category | flops | bytes accessed | tf_op | source)
XLA Modules:
  0.0 443.5 jit_solution(8854764190640074062)
XLA Ops:
  6.5 5.5 %fusion.10 = bf16[384,4096]{1,0:T(8,128)(2,1)} fusion(bf16[384,4096]{1,0:T(8,128)(2,1)} %param.9), kind=kLoop, calls=%fused_computation.17 | loop fusion | flops 9437184 | bytes 6291456 | tf_op jit(solution)/shard_map/convert_element_type | solution.py:31
  12.0 4.7 %copy.18 = bf16[384,4096]{0,1:T(8,128)(2,1)} copy(bf16[384,4096]{1,0:T(8,128)(2,1)} %fusion.10) | data formatting | bytes 6291456 | tf_op jit(solution)/shard_map/reshape | solution.py:31
  16.7 4.2 fusion.15
  21.0 230.2 %all-gather.6.cloned.1.call-done = f32[256,128,128]{2,1,0:T(8,128)} async-done(((f32[32,128,128]{2,1,0:T(8,128)}), f32[256,128,128]{2,1,0:T(8,128)}) %all-gather.6.cloned.1.call-update) | async-done | bytes 16777232 | tf_op jit(solution)/shard_map/all_gather | solution.py:12
  251.1 0.7 all-reduce.2.cloned.1.call-update
  251.9 0.0 all-gather.4.cloned.1.call-start
  251.9 104.1 %all-reduce.2.cloned.1.call-done = f32[1,32,128,128]{3,2,1,0:T(8,128)} async-done(((f32[1,32,128,128]{3,2,1,0:T(8,128)}), f32[1,32,128,128]{3,2,1,0:T(8,128)}) %all-reduce.2.cloned.1.call-update) | async-done | bytes 2097168 | tf_op jit(solution)/shard_map/psum | solution.py:36
  356.2 9.2 %fusion = f32[32,384,128]{1,2,0:T(8,128)} fusion(pred[384,384]{1,0:T(8,128)(4,1)S(1)} %iota_compare_fusion, bf16[384,32,128]{0,2,1:T(8,128)(2,1)} %bitcast.58, bf16[384,4096]{1,0:T(8,128)(2,1)S(1)} %copy-done, bf16[384,4096]{1,0:T(8,128)(2,1)} %param.8), kind=kOutput, calls=%fused_computation.3 | convolution fusion | flops 2434793472 | bytes 15876096 | tf_op jit(solution)/shard_map/hts,she->the/dot_general | solution.py:43
  365.4 28.6 %while.29 = (s32[]{:T(128)}, f32[32,128,128]{2,1,0:T(8,128)}, s32[]{:T(128)}, f32[8,32,128,128]{3,2,1,0:T(8,128)}, s32[]{:T(128)}, /*index=5*/s32[]{:T(128)}) while((s32[]{:T(128)}, f32[32,128,128]{2,1,0:T(8,128)}, s32[]{:T(128)}, f32[8,32,128,128]{3,2,1,0:T(8,128)}, s32[]{:T(128)}, /*index=5*/s32[]{:T(128)}) %tuple.73), condition=%wide.region_4.5_spmd.clone, body=%wide.region_3.4_spmd.clone.sunk | while | flops 1572868 | bytes 6291557 | solution.py:19
  365.4 3.9 add_select_fusion.5
  369.3 4.2 add_select_fusion.5
  373.5 4.1 add_select_fusion.5
  377.6 4.1 add_select_fusion.5
  381.7 4.1 add_select_fusion.5
  385.7 4.2 add_select_fusion.5
  389.9 4.1 add_select_fusion.5
  394.0 21.2 %all-gather.4.cloned.1.call-done = f32[4,32,128,128]{3,2,1,0:T(8,128)} async-done(((f32[1,32,128,128]{3,2,1,0:T(8,128)}), f32[4,32,128,128]{3,2,1,0:T(8,128)}) %all-gather.4.cloned.1.call-update) | async-done | bytes 8388624 | tf_op jit(solution)/shard_map/all_gather | solution.py:12
  415.2 7.0 %while.28 = (s32[]{:T(128)}, f32[32,128,128]{2,1,0:T(8,128)S(1)}, s32[]{:T(128)}, f32[4,32,128,128]{3,2,1,0:T(8,128)}, s32[]{:T(128)}, /*index=5*/s32[]{:T(128)}) while((s32[]{:T(128)}, f32[32,128,128]{2,1,0:T(8,128)S(1)}, s32[]{:T(128)}, f32[4,32,128,128]{3,2,1,0:T(8,128)}, s32[]{:T(128)}, /*index=5*/s32[]{:T(128)}) %tuple.72), condition=%wide.region_2.3_spmd.clone, body=%wide.region_1.2_spmd.clone.sunk | while | flops 1572868 | bytes 6291557 | solution.py:19
  415.2 2.3 add_select_fusion.4
  417.5 2.3 add_select_fusion.4
  419.9 2.3 add_select_fusion.4
  422.2 7.4 %multiply_reduce_fusion = (f32[384,32]{0,1:T(8,128)S(1)}, f32[32,128,384]{2,1,0:T(8,128)S(1)}) fusion(f32[32,384,128]{1,2,0:T(8,128)} %fusion, f32[32,128,128]{2,1,0:T(8,128)S(1)} %get-tuple-element.163, f32[32,128,128]{2,1,0:T(8,128)} %get-tuple-element.164, bf16[384,4096]{1,0:T(8,128)(2,1)} %param.8), kind=kOutput, calls=%fused_computation.20 | convolution fusion | flops 417845248 | bytes 19972096 | tf_op jit(solution)/shard_map/thd,hde->the/dot_general | solution.py:44
  429.7 2.5 multiply_convert_fusion
  432.2 4.8 %copy.16 = bf16[384,4096]{1,0:T(8,128)(2,1)} copy(bf16[384,4096]{0,1:T(8,128)(2,1)} %bitcast.59) | data formatting | bytes 6291456 | tf_op jit(solution)/shard_map/convert_element_type | solution.py:51
  (22 shorter events, 0.1 us)
Async XLA Ops:
  6.5 10.2 %copy-start = (bf16[384,4096]{1,0:T(8,128)(2,1)S(1)}, bf16[384,4096]{1,0:T(8,128)(2,1)}, u32[]{:S(2)}) copy-start(bf16[384,4096]{1,0:T(8,128)(2,1)} %param.10) | copy-start | bytes 9437188
  6.5 244.6 %all-gather.6.cloned.1.call-start = ((), (), s32[]{:S(2)}) async-start(), calls=%async_computation.2 | async-start | bytes 18874368 | tf_op jit(solution)/shard_map/all_gather | solution.py:12
  20.9 335.2 %copy-start.3 = (bf16[4096]{0:T(1024)(128)(2,1)S(1)}, bf16[4096]{0:T(1024)(128)(2,1)}, u32[]{:S(2)}) copy-start(bf16[4096]{0:T(1024)(128)(2,1)} %param.11) | copy-start | bytes 24580
  251.1 104.9 %all-reduce.2.cloned.1.call-start = ((), (), s32[]{:S(2)}) async-start(), calls=%async_computation | async-start | bytes 4194304 | tf_op jit(solution)/shard_map/psum | solution.py:36
  251.9 163.3 %all-gather.4.cloned.1.call-start = ((), (), s32[]{:S(2)}) async-start(), calls=%async_computation.1 | async-start | bytes 10485760 | tf_op jit(solution)/shard_map/all_gather | solution.py:12
  365.4 49.8 %copy-start.2 = (f32[32,128,128]{2,1,0:T(8,128)S(1)}, f32[32,128,128]{2,1,0:T(8,128)}, u32[]{:S(2)}) copy-start(f32[32,128,128]{2,1,0:T(8,128)} %custom-call) | copy-start | bytes 6291460
  422.2 7.5 %slice-start = ((s8[6291456]{0:T(1024)(128)(4,1)}), s8[4194304]{0:T(1024)(128)(4,1)S(1)}, s32[]{:S(2)}) async-start(s8[6291456]{0:T(1024)(128)(4,1)} %bitcast.61), calls=%async_computation.3 | async-start | bytes 8388608
  422.2 7.5 %slice-start.1 = ((s8[6291456]{0:T(1024)(128)(4,1)}), s8[2097152]{0:T(1024)(128)(4,1)S(1)}, s32[]{:S(2)}) async-start(s8[6291456]{0:T(1024)(128)(4,1)} %bitcast.61), calls=%async_computation.4 | async-start | bytes 4194304
  432.2 4.8 %copy-start.1 = (bf16[384,4096]{1,0:T(8,128)(2,1)S(1)}, bf16[384,4096]{1,0:T(8,128)(2,1)}, u32[]{:S(2)}) copy-start(bf16[384,4096]{1,0:T(8,128)(2,1)} %param.10) | copy-start | bytes 9437188
Sparse Core Ops, SparseCore 0:
  21.1 229.9 all-gather.5
  255.6 100.4 all-reduce.1
  357.6 57.5 all-gather.3
where the time goes:
time: 444 us; the launch traced here: 443 us
  waiting for transfers between devices  356 us (80%)
  other arithmetic  43.6 us (10%)
  matrix products  20.9 us (5%)
  between operations  13.2 us (3%)
  local copies, waits for them, and re-layouts  9.5 us (2%)
    all_gather x2, waiting for transfers between devices, entering(): pieces = lax.all_gather(value, axis)  251 us
    psum x1, waiting for transfers between devices, shards(): total = lax.psum(local, 'seq')  104 us
    select_n x10, other arithmetic, lap(): return jnp.where(position < mine, longer, subtotal)  35.5 us
    dot_general x1, matrix products, shards(): jnp.einsum('hts,she->the', scores, vals, preferred_element_type=jnp.float32)  9.23 us
  transfers between devices with their start and end apart: 3, of which 3 were waited for; matrix products, arithmetic and copies ran while one was open for 9% of the time, Pallas kernels for 0%

commit v1 on v0

--- a/solution.py
+++ b/solution.py
@@ -33,7 +33,9 @@
     local = jnp.einsum("thd,the->hde", fk, vals, preferred_element_type=jnp.float32)
     empty = jnp.zeros((HEADS, HEAD_DIM, HEAD_DIM), jnp.float32)
     within = entering(local, "seq", combine_sum, empty)
-    total = lax.psum(local, "seq")
+    total = local
+    for hop in (1, 2, 4):
+        total = total + lax.ppermute(total, "seq", [(dev, dev ^ hop) for dev in range(8)])
     before = entering(total, "grp", combine_sum, empty)
     carried = before + within
     positions = jnp.arange(rows, dtype=jnp.int32)

time: 444 us -> 539 us (1.21)
  waiting for transfers between devices: 356 us -> 447 us
  starting transfers between devices: 0.04 us -> 7.69 us
    ppermute x0 -> x3, waiting for transfers between devices: none -> 180 us  [shards(): lax.ppermute(total, 'seq', [(dev, dev ^ hop) for dev in range(8)])]
    psum x1 -> x0, waiting for transfers between devices: 104 us -> none  [shards(): total = lax.psum(local, 'seq')]
    all_gather x2, waiting for transfers between devices: 251 us -> 266 us  [entering(): pieces = lax.all_gather(value, axis)]
    ppermute x0 -> x3, starting transfers between devices: none -> 7.47 us  [shards(): lax.ppermute(total, 'seq', [(dev, dev ^ hop) for dev in range(8)])]
    select_n x10, other arithmetic: 35.5 us -> 28.3 us  [lap(): return jnp.where(position < mine, longer, subtotal)]
  transfers between devices with their start and end apart: 3 -> 5, of which waited for: 3 -> 5; matrix products, arithmetic and copies ran while one was open for 9% -> 4% of each run, Pallas kernels for 0% -> 0%
where the time goes in v1:
time: 539 us
  waiting for transfers between devices  447 us (83%)
  other arithmetic  40.1 us (7%)
  matrix products  20.8 us (4%)
  between operations  13.5 us (3%)
  local copies, waits for them, and re-layouts  9.48 us (2%)
  starting transfers between devices  7.69 us (1%)
    all_gather x2, waiting for transfers between devices, entering(): pieces = lax.all_gather(value, axis)  266 us
    ppermute x3, waiting for transfers between devices, shards(): lax.ppermute(total, 'seq', [(dev, dev ^ hop) for dev in range(8)])  180 us
    select_n x10, other arithmetic, lap(): return jnp.where(position < mine, longer, subtotal)  28.3 us
  transfers between devices with their start and end apart: 5, of which 5 were waited for; matrix products, arithmetic and copies ran while one was open for 4% of the time, Pallas kernels for 0%

profile of v1, /device:TPU:0, one launch (start us, length us, event | category | flops | bytes accessed | tf_op | source)
XLA Modules:
  0.0 538.9 jit_solution(10502233655606403979)
XLA Ops:
  6.5 5.5 %fusion.10 = bf16[384,4096]{1,0:T(8,128)(2,1)} fusion(bf16[384,4096]{1,0:T(8,128)(2,1)} %param.9), kind=kLoop, calls=%fused_computation.17 | loop fusion | flops 9437184 | bytes 6291456 | tf_op jit(solution)/shard_map/convert_element_type | solution.py:31
  12.0 4.7 copy.18
  16.7 4.2 fusion.15
  20.9 3.0 collective-permute-start
  23.9 45.8 %collective-permute-done = f32[32,128,128]{2,1,0:T(8,128)S(1)} collective-permute-done((f32[32,128,128]{2,1,0:T(8,128)}, f32[32,128,128]{2,1,0:T(8,128)S(1)}, u32[]{:S(2)}, u32[]{:S(2)}) %collective-permute-start) | collective-permute-done | bytes 2097184 | tf_op jit(solution)/shard_map/ppermute | solution.py:38
  73.5 45.0 %collective-permute-done.1 = f32[32,128,128]{2,1,0:T(8,128)S(1)} collective-permute-done((f32[32,128,128]{2,1,0:T(8,128)S(1)}, f32[32,128,128]{2,1,0:T(8,128)S(1)}, u32[]{:S(2)}, u32[]{:S(2)}) %collective-permute-start.1) | collective-permute-done | bytes 2097184 | tf_op jit(solution)/shard_map/ppermute | solution.py:38
  118.8 2.6 collective-permute-start.2
  121.4 89.2 %collective-permute-done.2 = f32[32,128,128]{2,1,0:T(8,128)S(1)} collective-permute-done((f32[32,128,128]{2,1,0:T(8,128)S(1)}, f32[32,128,128]{2,1,0:T(8,128)S(1)}, u32[]{:S(2)}, u32[]{:S(2)}) %collective-permute-start.2) | collective-permute-done | bytes 2097184 | tf_op jit(solution)/shard_map/ppermute | solution.py:38
  213.1 9.2 %fusion = f32[32,384,128]{1,2,0:T(8,128)} fusion(pred[384,384]{1,0:T(8,128)(4,1)S(1)} %iota_compare_fusion, bf16[384,32,128]{0,2,1:T(8,128)(2,1)} %bitcast.58, bf16[384,4096]{1,0:T(8,128)(2,1)S(1)} %copy-done, bf16[384,4096]{1,0:T(8,128)(2,1)} %param.8), kind=kOutput, calls=%fused_computation.3 | convolution fusion | flops 2434793472 | bytes 15876096 | tf_op jit(solution)/shard_map/hts,she->the/dot_general | solution.py:45
  222.3 49.1 %all-gather.5.cloned.1.call-done = f32[128,128,128]{2,1,0:T(8,128)} async-done(((f32[32,128,128]{2,1,0:T(8,128)}), f32[128,128,128]{2,1,0:T(8,128)}) %all-gather.5.cloned.1.call-update) | async-done | bytes 8388624 | tf_op jit(solution)/shard_map/all_gather | solution.py:12
  271.5 12.1 %while.28 = (s32[]{:T(128)}, f32[32,128,128]{2,1,0:T(8,128)}, s32[]{:T(128)}, f32[4,32,128,128]{3,2,1,0:T(8,128)}, s32[]{:T(128)}, /*index=5*/s32[]{:T(128)}) while((s32[]{:T(128)}, f32[32,128,128]{2,1,0:T(8,128)}, s32[]{:T(128)}, f32[4,32,128,128]{3,2,1,0:T(8,128)}, s32[]{:T(128)}, /*index=5*/s32[]{:T(128)}) %tuple.71), condition=%wide.region_1.2_spmd.clone, body=%wide.region_0.1_spmd.clone.sunk | while | flops 1572868 | bytes 6291549 | solution.py:19
  271.5 3.6 add_select_fusion.4
  275.0 4.0 add_select_fusion.4
  279.1 4.5 add_select_fusion.4
  283.5 217.4 %all-gather.7.cloned.1.call-done = f32[256,128,128]{2,1,0:T(8,128)} async-done(((f32[32,128,128]{2,1,0:T(8,128)}), f32[256,128,128]{2,1,0:T(8,128)}) %all-gather.7.cloned.1.call-update) | async-done | bytes 16777232 | tf_op jit(solution)/shard_map/all_gather | solution.py:12
  500.9 16.3 %while.29 = (s32[]{:T(128)}, f32[32,128,128]{2,1,0:T(8,128)S(1)}, s32[]{:T(128)}, f32[8,32,128,128]{3,2,1,0:T(8,128)}, s32[]{:T(128)}, /*index=5*/s32[]{:T(128)}) while((s32[]{:T(128)}, f32[32,128,128]{2,1,0:T(8,128)S(1)}, s32[]{:T(128)}, f32[8,32,128,128]{3,2,1,0:T(8,128)}, s32[]{:T(128)}, /*index=5*/s32[]{:T(128)}) %tuple.72), condition=%wide.region_3.4_spmd.clone, body=%wide.region_2.3_spmd.clone.sunk | while | flops 1572868 | bytes 6291549 | solution.py:19
  503.2 2.3 add_select_fusion.5
  505.6 2.3 add_select_fusion.5
  507.9 2.3 add_select_fusion.5
  510.2 2.3 add_select_fusion.5
  514.9 2.3 add_select_fusion.5
  517.3 7.4 %multiply_reduce_fusion = (f32[384,32]{0,1:T(8,128)S(1)}, f32[32,128,384]{2,1,0:T(8,128)S(1)}) fusion(f32[32,384,128]{1,2,0:T(8,128)} %fusion, f32[32,128,128]{2,1,0:T(8,128)} %get-tuple-element.163, f32[32,128,128]{2,1,0:T(8,128)S(1)} %get-tuple-element.164, bf16[384,4096]{1,0:T(8,128)(2,1)} %param.8), kind=kOutput, calls=%fused_computation.20 | convolution fusion | flops 417845248 | bytes 19972096 | tf_op jit(solution)/shard_map/thd,hde->the/dot_general | solution.py:46
  524.8 2.5 multiply_convert_fusion
  527.2 4.8 copy.16
  (28 shorter events, 11.1 us)
Async XLA Ops:
  6.5 10.2 %copy-start = (bf16[384,4096]{1,0:T(8,128)(2,1)S(1)}, bf16[384,4096]{1,0:T(8,128)(2,1)}, u32[]{:S(2)}) copy-start(bf16[384,4096]{1,0:T(8,128)(2,1)} %param.10) | copy-start | bytes 9437188
  6.5 264.9 %all-gather.5.cloned.1.call-start = ((), (), s32[]{:S(2)}) async-start(), calls=%async_computation | async-start | bytes 10485760 | tf_op jit(solution)/shard_map/all_gather | solution.py:12
  20.9 48.8 %collective-permute-start = (f32[32,128,128]{2,1,0:T(8,128)}, f32[32,128,128]{2,1,0:T(8,128)S(1)}, u32[]{:S(2)}, u32[]{:S(2)}) collective-permute-start(f32[32,128,128]{2,1,0:T(8,128)} %fusion.15), channel_id=1, source_target_pairs={{0,1},{1,0},{2,3},{3,2},{4,5},{5,4},{6,7},{7,6},{8,9},{9,8},{10,11... | collective-permute-start | bytes 6291464 | tf_op jit(solution)/shard_map/ppermute | solution.py:38
  71.6 46.9 %collective-permute-start.1 = (f32[32,128,128]{2,1,0:T(8,128)S(1)}, f32[32,128,128]{2,1,0:T(8,128)S(1)}, u32[]{:S(2)}, u32[]{:S(2)}) collective-permute-start(f32[32,128,128]{2,1,0:T(8,128)S(1)} %add.91), channel_id=1, source_target_pairs={{0,2},{1,3},{2,0},{3,1},{4,6},{5,7},{6,4},{7,5},{8,10},{9,11},{10,... | collective-permute-start | bytes 6291464 | tf_op jit(solution)/shard_map/ppermute | solution.py:38
  118.8 91.8 %collective-permute-start.2 = (f32[32,128,128]{2,1,0:T(8,128)S(1)}, f32[32,128,128]{2,1,0:T(8,128)S(1)}, u32[]{:S(2)}, u32[]{:S(2)}) collective-permute-start(f32[32,128,128]{2,1,0:T(8,128)S(1)} %add.92), channel_id=1, source_target_pairs={{0,4},{1,5},{2,6},{3,7},{4,0},{5,1},{6,2},{7,3},{8,12},{9,13},{10,... | collective-permute-start | bytes 6291464 | tf_op jit(solution)/shard_map/ppermute | solution.py:38
  212.2 0.9 copy-start.3
  212.2 288.7 %all-gather.7.cloned.1.call-start = ((), (), s32[]{:S(2)}) async-start(), calls=%async_computation.1 | async-start | bytes 18874368 | tf_op jit(solution)/shard_map/all_gather | solution.py:12
  271.5 229.4 %copy-start.2 = (f32[32,128,128]{2,1,0:T(8,128)S(1)}, f32[32,128,128]{2,1,0:T(8,128)}, u32[]{:S(2)}) copy-start(f32[32,128,128]{2,1,0:T(8,128)} %custom-call.1) | copy-start | bytes 6291460
  517.2 7.5 %slice-start = ((s8[6291456]{0:T(1024)(128)(4,1)}), s8[4194304]{0:T(1024)(128)(4,1)S(1)}, s32[]{:S(2)}) async-start(s8[6291456]{0:T(1024)(128)(4,1)} %bitcast.61), calls=%async_computation.2 | async-start | bytes 8388608
  517.3 7.5 %slice-start.1 = ((s8[6291456]{0:T(1024)(128)(4,1)}), s8[2097152]{0:T(1024)(128)(4,1)S(1)}, s32[]{:S(2)}) async-start(s8[6291456]{0:T(1024)(128)(4,1)} %bitcast.61), calls=%async_computation.3 | async-start | bytes 4194304
  527.2 4.8 copy-start.1
Sparse Core Ops, SparseCore 0:
  212.4 59.0 all-gather.4
  273.6 227.2 all-gather.6
